TPU v7x, 32 devices: a whole 2x2x4 slice. The times are simulated.
32 devices in a mesh: row: 4 (over z), col: 8 (over y, x, core).
Axes of the slice: x: 2, y: 2, z: 4, core: 2. Of those that a mesh axis runs over, the one named last changes fastest.
Arguments:
- activations: bfloat16 [256, 256, 384], P('row', 'col'), may hold values from -6 to 6
- cotangent: bfloat16 [256, 256, 384], P('row', 'col'), may hold values from -6 to 6
- first_gain: float32 [384], replicated, may hold values from 0.1 to 1.9
- joint_weight: bfloat16 [384, 1152], replicated, may hold values from -4 to 4, as said below
- output_weight: bfloat16 [384, 384], replicated, may hold values from -0.3125 to 0.3125
- second_gain: float32 [384], replicated, may hold values from 0.1 to 1.9
- expand_weight: bfloat16 [384, 1536], replicated, may hold values from -0.3125 to 0.3125
- reduce_weight: bfloat16 [1536, 384], replicated, may hold values from -0.15625 to 0.15625
Outputs:
- block_out: bfloat16 [256, 256, 384], P('row', 'col')
- grad_input: bfloat16 [256, 256, 384], P('row', 'col')
- grad_joint: float32 [384, 1152], replicated
- grad_project: float32 [384, 384], replicated
- grad_expand: float32 [384, 1536], replicated
- grad_reduce: float32 [1536, 384], replicated
- grad_first_gain: float32 [384], replicated
- grad_second_gain: float32 [384], replicated
Inputs may be any that keep to these rules, and one draw needn't show every extreme that they name: `joint_weight`: Queries, keys and values side by side along the columns, each 384 wide, heads of 32 consecutive columns.
All inputs are finite; a program needn't handle non-finite values.
Results may differ from a plain program's by a relative error of at most 0.014.
The roundings to bfloat16 on the way count: a program that leaves them out, or rounds other values in their place, can miss the bound.
Values may be sent and summed in bfloat16 or wider, within the bound.
No kernel may reach another device: no remote copies, remote signals or barrier semaphores. Data moves between devices by JAX's collectives and lax.ppermute only.
A program may use at most 192 MiB of HBM per device.

v0:
```python
import jax
import jax.numpy as jnp
from jax import lax
from jax.sharding import PartitionSpec as P

HEADS = 12
GRID = 16


EPSILON = 1e-05
SQRT_HALF = 0.7071067811865476
INV_ROOT_TAU = 0.3989422804014327


def normalize(values):
    center = values - jnp.mean(values, axis=-1, keepdims=True)
    inv_std = lax.rsqrt(jnp.mean(center * center, axis=-1, keepdims=True) + EPSILON)
    return (center * inv_std, inv_std)


def norm_back(grad_norm, gain_vec, normed, inv_std):
    scaled = grad_norm * gain_vec
    return inv_std * (
        scaled
        - jnp.mean(scaled, axis=-1, keepdims=True)
        - normed * jnp.mean(scaled * normed, axis=-1, keepdims=True)
    )


def gelu_value(pre_act):
    return 0.5 * pre_act * (1.0 + jax.scipy.special.erf(pre_act * SQRT_HALF))


def gelu_slope(pre_act):
    return (
        0.5 * (1.0 + jax.scipy.special.erf(pre_act * SQRT_HALF))
        + pre_act * jnp.exp(-0.5 * pre_act * pre_act) * INV_ROOT_TAU
    )


def project_rows(inputs, gain_vec, weight):
    normed, inv_std = normalize(inputs)
    scaled = (normed * gain_vec).astype(jnp.bfloat16)
    triple = jnp.dot(scaled, weight, preferred_element_type=jnp.float32).astype(jnp.bfloat16)
    return (triple, scaled, normed, inv_std)


def split_heads(rows, feature_dim):
    return rows.reshape(rows.shape[0], rows.shape[1], HEADS, feature_dim // HEADS)


def attend(triple):
    feature_dim = triple.shape[-1] // 3
    queries = split_heads(triple[..., :feature_dim], feature_dim)
    key_rows = split_heads(triple[..., feature_dim : 2 * feature_dim], feature_dim)
    value_rows = split_heads(triple[..., 2 * feature_dim :], feature_dim)
    score_scale = (feature_dim // HEADS) ** (-0.5)
    scores = (
        jnp.einsum("bqhe,bkhe->bhqk", queries, key_rows, preferred_element_type=jnp.float32)
        * score_scale
    )
    row_max = jnp.max(scores, axis=-1, keepdims=True)
    weights = jnp.exp(scores - row_max)
    weights = weights / jnp.sum(weights, axis=-1, keepdims=True)
    return (weights, queries, key_rows, value_rows, score_scale)


def attend_forward(triple):
    weights, queries, key_rows, value_rows, score_scale = attend(triple)
    mixed_rows = jnp.einsum(
        "bhqk,bkhe->bqhe",
        weights.astype(jnp.bfloat16),
        value_rows,
        preferred_element_type=jnp.float32,
    ).astype(jnp.bfloat16)
    return mixed_rows.reshape(triple.shape[0], triple.shape[1], -1)


def attend_backward(triple, grad_mixed):
    weights, queries, key_rows, value_rows, score_scale = attend(triple)
    feature_dim = triple.shape[-1] // 3
    grad_heads = split_heads(grad_mixed, feature_dim)
    grad_weights = jnp.einsum(
        "bqhe,bkhe->bhqk", grad_heads, value_rows, preferred_element_type=jnp.float32
    )
    inner_sum = jnp.sum(weights * grad_weights, axis=-1, keepdims=True)
    grad_scores = (weights * (grad_weights - inner_sum) * score_scale).astype(jnp.bfloat16)
    grad_query = jnp.einsum(
        "bhqk,bkhe->bqhe", grad_scores, key_rows, preferred_element_type=jnp.float32
    ).astype(jnp.bfloat16)
    grad_key = jnp.einsum(
        "bhqk,bqhe->bkhe", grad_scores, queries, preferred_element_type=jnp.float32
    ).astype(jnp.bfloat16)
    grad_value = jnp.einsum(
        "bhqk,bqhe->bkhe",
        weights.astype(jnp.bfloat16),
        grad_heads,
        preferred_element_type=jnp.float32,
    ).astype(jnp.bfloat16)
    shape_out = (triple.shape[0], triple.shape[1], feature_dim)
    return jnp.concatenate(
        [grad_query.reshape(shape_out), grad_key.reshape(shape_out), grad_value.reshape(shape_out)],
        axis=-1,
    )


def by_blocks(function, operands):
    groups = operands[0].shape[0]
    per_step = 2
    stacked = tuple(
        (
            operand.reshape((groups // per_step, per_step) + operand.shape[1:])
            for operand in operands
        )
    )
    result = lax.map(lambda pieces: function(*pieces), stacked)
    return result.reshape((groups,) + result.shape[2:])


def tail_back(inputs, mixed_rows, out_weight, gain_vec, up_weight, down_weight, cot_rows):
    attended = inputs + jnp.dot(mixed_rows, out_weight, preferred_element_type=jnp.float32)
    normed, inv_std = normalize(attended)
    scaled = (normed * gain_vec).astype(jnp.bfloat16)
    pre_act = jnp.dot(scaled, up_weight, preferred_element_type=jnp.float32)
    hidden = gelu_value(pre_act).astype(jnp.bfloat16)
    result = (attended + jnp.dot(hidden, down_weight, preferred_element_type=jnp.float32)).astype(
        jnp.bfloat16
    )
    grad_down = jnp.einsum("nf,nd->fd", hidden, cot_rows, preferred_element_type=jnp.float32)
    grad_hidden = jnp.einsum(
        "nd,fd->nf", cot_rows, down_weight, preferred_element_type=jnp.float32
    ).astype(jnp.bfloat16)
    grad_pre = (grad_hidden * gelu_slope(pre_act)).astype(jnp.bfloat16)
    grad_up = jnp.einsum("nd,nf->df", scaled, grad_pre, preferred_element_type=jnp.float32)
    grad_scaled = jnp.einsum("nf,df->nd", grad_pre, up_weight, preferred_element_type=jnp.float32)
    grad_gain = jnp.sum(grad_scaled * normed, axis=0)
    grad_attended = cot_rows.astype(jnp.float32) + norm_back(grad_scaled, gain_vec, normed, inv_std)
    grad_attended_b = grad_attended.astype(jnp.bfloat16)
    grad_out = jnp.einsum(
        "nd,ne->de", mixed_rows, grad_attended_b, preferred_element_type=jnp.float32
    )
    grad_mixed = jnp.einsum(
        "ne,de->nd", grad_attended_b, out_weight, preferred_element_type=jnp.float32
    ).astype(jnp.bfloat16)
    tail_grads = (grad_out, grad_gain, grad_up, grad_down)
    return (result, grad_attended, grad_mixed, tail_grads)


def head_back(normed, inv_std, scaled, gain_vec, weight, grad_triple, grad_attended):
    grad_joint = jnp.einsum("nd,nt->dt", scaled, grad_triple, preferred_element_type=jnp.float32)
    grad_scaled = jnp.einsum("nt,dt->nd", grad_triple, weight, preferred_element_type=jnp.float32)
    grad_gain = jnp.sum(grad_scaled * normed, axis=0)
    grad_input = (grad_attended + norm_back(grad_scaled, gain_vec, normed, inv_std)).astype(
        jnp.bfloat16
    )
    return (grad_input, (grad_joint, grad_gain))


def shards(
    activations,
    cotangent,
    first_gain,
    joint_weight,
    output_weight,
    second_gain,
    expand_weight,
    reduce_weight,
):
    row_devs = lax.axis_size("row")
    col_devs = lax.axis_size("col")
    tile_rows, tile_cols, channels = activations.shape
    local_rows = GRID // row_devs
    local_cols = GRID // col_devs
    stride_rows = tile_rows // local_rows
    stride_cols = tile_cols // local_cols
    part_rows = stride_rows // row_devs
    part_cols = stride_cols // col_devs
    tokens = GRID * GRID
    factor = float(tile_rows * tile_cols * row_devs * col_devs) ** (-0.5)

    def to_layout(tile):
        return tile.reshape(
            local_rows, stride_rows, local_cols, stride_cols, tile.shape[-1]
        ).transpose(1, 3, 0, 2, 4)

    def regroup(grouped):
        return grouped.reshape(part_rows, part_cols, GRID, GRID, grouped.shape[-1])

    def from_layout(arrived):
        return arrived.transpose(2, 0, 3, 1, 4).reshape(tile_rows, tile_cols, arrived.shape[-1])

    arrived_pair = (
        lax.all_to_all(
            lax.all_to_all(to_layout(activations), "row", split_axis=0, concat_axis=2, tiled=True),
            "col",
            split_axis=1,
            concat_axis=3,
            tiled=True,
        ),
        lax.all_to_all(
            lax.all_to_all(to_layout(cotangent), "row", split_axis=0, concat_axis=2, tiled=True),
            "col",
            split_axis=1,
            concat_axis=3,
            tiled=True,
        ),
    )
    inputs = arrived_pair[0].reshape(-1, channels).astype(jnp.float32)
    cot_rows = arrived_pair[1].reshape(-1, channels)
    triple, scaled_first, normed_first, inv_first = project_rows(inputs, first_gain, joint_weight)
    triple_grp = triple.reshape(-1, tokens, 3 * channels)
    mixed_rows = by_blocks(attend_forward, (triple_grp,)).reshape(-1, channels)
    result, grad_attended, grad_mixed, tail_grads = tail_back(
        inputs, mixed_rows, output_weight, second_gain, expand_weight, reduce_weight, cot_rows
    )
    grad_triple = by_blocks(
        attend_backward, (triple_grp, grad_mixed.reshape(-1, tokens, channels))
    ).reshape(-1, 3 * channels)
    grad_input, head_grads = head_back(
        normed_first, inv_first, scaled_first, first_gain, joint_weight, grad_triple, grad_attended
    )
    returned = (
        lax.all_to_all(
            lax.all_to_all(
                regroup(result.reshape(-1, tokens, channels)),
                "row",
                split_axis=2,
                concat_axis=0,
                tiled=True,
            ),
            "col",
            split_axis=3,
            concat_axis=1,
            tiled=True,
        ),
        lax.all_to_all(
            lax.all_to_all(
                regroup(grad_input.reshape(-1, tokens, channels)),
                "row",
                split_axis=2,
                concat_axis=0,
                tiled=True,
            ),
            "col",
            split_axis=3,
            concat_axis=1,
            tiled=True,
        ),
    )
    block_out = from_layout(returned[0])
    grad_in_tile = from_layout(returned[1])
    grad_out, grad_second, grad_up, grad_down = tail_grads
    grad_joint, grad_first = head_grads
    summed = lax.psum(
        (grad_joint, grad_out, grad_up, grad_down, grad_first, grad_second), ("row", "col")
    )
    return (block_out, grad_in_tile) + tuple((summand * factor for summand in summed))


def solution(mesh):
    placed = (P("row", "col", None), P("row", "col", None), P(), P(), P(), P(), P(), P())
    return jax.shard_map(
        shards,
        mesh=mesh,
        in_specs=placed,
        out_specs=(P("row", "col", None), P("row", "col", None), P(), P(), P(), P(), P(), P()),
        check_vma=False,
    )
```

profile of v0, /device:TPU:0, one launch (start us, length us, event | category | flops | bytes accessed | tf_op | source)
XLA Modules:
  0.0 676.4 jit_solution(6939337770541259903)
XLA Ops:
  19.2 34.2 %all-to-all-done = bf16[16,16,4,2,384]{4,1,3,2,0:T(8,128)(2,1)S(1)} async-done(((bf16[16,16,4,2,384]{4,1,3,2,0:T(8,128)(2,1)}), bf16[16,16,4,2,384]{4,1,3,2,0:T(8,128)(2,1)S(1)}, u32[]{:S(2)}, u32[]{:S(2)}) %all-to-all-start) | async-done | bytes 1572896 | tf_op jit(solution)/shard_map/all_to_all | solution.py:194
  62.3 32.3 %all-to-all-done.4 = bf16[16,16,4,2,384]{4,1,3,2,0:T(8,128)(2,1)S(1)} async-done(((bf16[16,16,4,2,384]{4,1,3,2,0:T(8,128)(2,1)}), bf16[16,16,4,2,384]{4,1,3,2,0:T(8,128)(2,1)S(1)}, u32[]{:S(2)}, u32[]{:S(2)}) %all-to-all-start.4) | async-done | bytes 1572896 | tf_op jit(solution)/shard_map/all_to_all | solution.py:201
  103.7 16.8 %all-to-all-done.1 = bf16[4,16,16,2,384]{4,3,2,0,1:T(2,128)(2,1)S(1)} async-done(((bf16[4,16,16,2,384]{4,3,2,0,1:T(2,128)(2,1)}), bf16[4,16,16,2,384]{4,3,2,0,1:T(2,128)(2,1)S(1)}, u32[]{:S(2)}, u32[]{:S(2)}) %all-to-all-start.1) | async-done | bytes 1572896 | tf_op jit(solution)/shard_map/all_to_all | solution.py:193
  155.2 7.2 %convolution_convert_fusion.1 = bf16[2048,1152]{1,0:T(8,128)(2,1)} fusion(bf16[384,1152]{1,0:T(8,128)(2,1)} %param.15, f32[2048,384]{1,0:T(8,128)} %reshape.160, f32[384]{0:T(512)S(1)} %copy-done.25, f32[2048]{0:T(1024)S(1)} %rsqrt.21, f32[2048]{0:T(1024)S(1)} %div.43), kind=kOutput, calls=%fused_computation.51 | convolution fusion | flops 1817444352 | bytes 8766976 | tf_op jit(solution)/shard_map/dot_general | solution.py:44
  162.4 6.6 copy.142
  169.1 52.6 %while.20 = (s32[]{:T(128)}, bf16[4,2,256,384]{3,2,1,0:T(8,128)(2,1)}, bf16[4,2,256,1152]{2,3,1,0:T(8,128)(2,1)}, s32[]{:T(128)}) while((s32[]{:T(128)}, bf16[4,2,256,384]{3,2,1,0:T(8,128)(2,1)}, bf16[4,2,256,1152]{2,3,1,0:T(8,128)(2,1)}, s32[]{:T(128)}) %tuple.70), condition=%wide.region_5.6_spmd, body=%wide.region_2.5_spmd.sunk | while | flops 209387776 | bytes 20496452 | solution.py:116
  184.3 6.5 fusion.129
  197.4 6.5 fusion.129
  210.5 6.5 fusion.129
  240.1 6.9 %fusion.50 = bf16[2048,1536]{1,0:T(8,128)(2,1)S(1)} fusion(f32[2048,1536]{1,0:T(8,128)S(1)} %get-tuple-element.130, bf16[2048,384]{1,0:T(8,128)(2,1)S(1)} %copy-done.7, bf16[1536,384]{1,0:T(8,128)(2,1)S(1)} %copy-done.28), kind=kOutput, calls=%fused_computation.47 | convolution fusion | flops 2453667840 | bytes 21626880 | tf_op jit(solution)/shard_map/nd,fd->nf/dot_general | solution.py:130
  277.3 145.1 %while.21 = (s32[]{:T(128)}, bf16[4,2,256,1152]{3,2,1,0:T(8,128)(2,1)}, bf16[4,2,256,1152]{2,3,1,0:T(8,128)(2,1)}, bf16[4,2,256,384]{3,2,1,0:T(8,128)(2,1)}, s32[]{:T(128)}) while((s32[]{:T(128)}, bf16[4,2,256,1152]{3,2,1,0:T(8,128)(2,1)}, bf16[4,2,256,1152]{2,3,1,0:T(8,128)(2,1)}, bf16[4,2,256,384]{3,2,1,0:T(8,128)(2,1)}, s32[]{:T(128)}) %tuple.79), condition=%wide.region_14.15_spmd, body=%wide.region_10.14_spmd.sunk | while | flops 537342720 | bytes 61440080 | solution.py:116
  288.6 10.0 %fusion.146 = bf16[2,12,32,256]{3,2,1,0:T(8,128)(2,1)S(1)} fusion(bf16[2,256,12,32]{1,3,2,0:T(8,128)(2,1)S(1)} %bitcast.175, f32[2,12,256,256]{2,3,1,0:T(8,128)} %fusion.144, f32[2,12,256,256]{2,3,1,0:T(8,128)} %get-tuple-element.196, f32[2,12,256]{2,1,0:T(8,128)S(1)} %get-tuple-element.197), kind=kOutput, calls=%fused_computation.29.clone.1 | convolution fusion | flops 111876352 | bytes 13393920 | tf_op jit(solution)/shard_map/while/body/eval_jaxpr/bhqk,bkhe->bqhe/dot_general | solution.py:88
  298.6 9.3 %fusion.145 = bf16[2,12,32,256]{3,2,1,0:T(8,128)(2,1)S(1)} fusion(bf16[2,256,12,32]{1,3,2,0:T(8,128)(2,1)S(1)} %bitcast.173, f32[2,12,256,256]{2,3,1,0:T(8,128)} %fusion.144, f32[2,12,256,256]{2,3,1,0:T(8,128)} %get-tuple-element.196, f32[2,12,256]{2,1,0:T(8,128)S(1)} %get-tuple-element.197), kind=kOutput, calls=%fused_computation.30.clone.1 | convolution fusion | flops 111876352 | bytes 13393920 | tf_op jit(solution)/shard_map/while/body/eval_jaxpr/bhqk,bqhe->bkhe/dot_general | solution.py:91
  324.8 10.0 %fusion.146 = bf16[2,12,32,256]{3,2,1,0:T(8,128)(2,1)S(1)} fusion(bf16[2,256,12,32]{1,3,2,0:T(8,128)(2,1)S(1)} %bitcast.175, f32[2,12,256,256]{2,3,1,0:T(8,128)} %fusion.144, f32[2,12,256,256]{2,3,1,0:T(8,128)} %get-tuple-element.196, f32[2,12,256]{2,1,0:T(8,128)S(1)} %get-tuple-element.197), kind=kOutput, calls=%fused_computation.29.clone.1 | convolution fusion | flops 111876352 | bytes 13393920 | tf_op jit(solution)/shard_map/while/body/eval_jaxpr/bhqk,bkhe->bqhe/dot_general | solution.py:88
  334.8 9.3 %fusion.145 = bf16[2,12,32,256]{3,2,1,0:T(8,128)(2,1)S(1)} fusion(bf16[2,256,12,32]{1,3,2,0:T(8,128)(2,1)S(1)} %bitcast.173, f32[2,12,256,256]{2,3,1,0:T(8,128)} %fusion.144, f32[2,12,256,256]{2,3,1,0:T(8,128)} %get-tuple-element.196, f32[2,12,256]{2,1,0:T(8,128)S(1)} %get-tuple-element.197), kind=kOutput, calls=%fused_computation.30.clone.1 | convolution fusion | flops 111876352 | bytes 13393920 | tf_op jit(solution)/shard_map/while/body/eval_jaxpr/bhqk,bqhe->bkhe/dot_general | solution.py:91
  361.1 10.0 %fusion.146 = bf16[2,12,32,256]{3,2,1,0:T(8,128)(2,1)S(1)} fusion(bf16[2,256,12,32]{1,3,2,0:T(8,128)(2,1)S(1)} %bitcast.175, f32[2,12,256,256]{2,3,1,0:T(8,128)} %fusion.144, f32[2,12,256,256]{2,3,1,0:T(8,128)} %get-tuple-element.196, f32[2,12,256]{2,1,0:T(8,128)S(1)} %get-tuple-element.197), kind=kOutput, calls=%fused_computation.29.clone.1 | convolution fusion | flops 111876352 | bytes 13393920 | tf_op jit(solution)/shard_map/while/body/eval_jaxpr/bhqk,bkhe->bqhe/dot_general | solution.py:88
  371.1 9.3 %fusion.145 = bf16[2,12,32,256]{3,2,1,0:T(8,128)(2,1)S(1)} fusion(bf16[2,256,12,32]{1,3,2,0:T(8,128)(2,1)S(1)} %bitcast.173, f32[2,12,256,256]{2,3,1,0:T(8,128)} %fusion.144, f32[2,12,256,256]{2,3,1,0:T(8,128)} %get-tuple-element.196, f32[2,12,256]{2,1,0:T(8,128)S(1)} %get-tuple-element.197), kind=kOutput, calls=%fused_computation.30.clone.1 | convolution fusion | flops 111876352 | bytes 13393920 | tf_op jit(solution)/shard_map/while/body/eval_jaxpr/bhqk,bqhe->bkhe/dot_general | solution.py:91
  397.3 10.0 %fusion.146 = bf16[2,12,32,256]{3,2,1,0:T(8,128)(2,1)S(1)} fusion(bf16[2,256,12,32]{1,3,2,0:T(8,128)(2,1)S(1)} %bitcast.175, f32[2,12,256,256]{2,3,1,0:T(8,128)} %fusion.144, f32[2,12,256,256]{2,3,1,0:T(8,128)} %get-tuple-element.196, f32[2,12,256]{2,1,0:T(8,128)S(1)} %get-tuple-element.197), kind=kOutput, calls=%fused_computation.29.clone.1 | convolution fusion | flops 111876352 | bytes 13393920 | tf_op jit(solution)/shard_map/while/body/eval_jaxpr/bhqk,bkhe->bqhe/dot_general | solution.py:88
  407.3 9.3 %fusion.145 = bf16[2,12,32,256]{3,2,1,0:T(8,128)(2,1)S(1)} fusion(bf16[2,256,12,32]{1,3,2,0:T(8,128)(2,1)S(1)} %bitcast.173, f32[2,12,256,256]{2,3,1,0:T(8,128)} %fusion.144, f32[2,12,256,256]{2,3,1,0:T(8,128)} %get-tuple-element.196, f32[2,12,256]{2,1,0:T(8,128)S(1)} %get-tuple-element.197), kind=kOutput, calls=%fused_computation.30.clone.1 | convolution fusion | flops 111876352 | bytes 13393920 | tf_op jit(solution)/shard_map/while/body/eval_jaxpr/bhqk,bqhe->bkhe/dot_general | solution.py:91
  432.0 7.3 %multiply_reduce_fusion.4 = (f32[384]{0:T(512)S(1)}, f32[2048]{0:T(1024)S(1)}, f32[2048]{0:T(1024)S(1)}, f32[2048,384]{1,0:T(8,128)S(1)}) fusion(f32[2048,384]{1,0:T(8,128)} %reshape.160, f32[2048]{0:T(1024)S(1)} %copy-done.21, f32[2048]{0:T(1024)S(1)} %copy-done.23, f32[384]{0:T(512)S(1)} %copy-done.26, bf16[2048,1152]{1,0:T(8,128)(2,1)} %bitcast.205, ...), kind=kOutput, calls=%fused_computation.54 | convolution fusion | flops 1818226304 | bytes 11930624 | tf_op jit(solution)/shard_map/nt,dt->nd/dot_general | solution.py:151
  451.0 49.4 %all-to-all-done.6 = bf16[4,2,16,16,384]{4,3,1,0,2:T(8,128)(2,1)S(1)} async-done(((bf16[4,2,16,16,384]{4,3,1,0,2:T(8,128)(2,1)}), bf16[4,2,16,16,384]{4,3,1,0,2:T(8,128)(2,1)S(1)}, u32[]{:S(2)}, u32[]{:S(2)}) %all-to-all-start.6) | async-done | bytes 1572896 | tf_op jit(solution)/shard_map/all_to_all | solution.py:237
  505.1 57.2 %all-reduce = (f32[384]{0:T(512)S(1)}, f32[384]{0:T(512)S(1)}) all-reduce(f32[384]{0:T(512)S(1)} %get-tuple-element.93, f32[384]{0:T(512)S(1)} %copy-done.27), channel_id=1, replica_groups=mesh['row'=4,'col'=8] {'row','col'}, use_global_device_ids=true, to_apply=%region_22.23 | all-reduce | flops 768 | bytes 6144 | tf_op jit(solution)/shard_map/psum | solution.py:254
  567.0 69.9 %all-reduce.4.cloned.1.call-done = (f32[384,1152]{1,0:T(8,128)}, f32[384,384]{1,0:T(8,128)}, f32[384,1536]{1,0:T(8,128)}, f32[1536,384]{1,0:T(8,128)}) async-done(((f32[384,1152]{1,0:T(8,128)}, f32[384,384]{1,0:T(8,128)}, f32[384,1536]{1,0:T(8,128)}, f32[1536,384]{1,0:T(8,128)}), (f32[384,1152]{1,0:T(8,128)}, f32[384,384]{1,0:T(8,128)}, f32[384,1536]{1,0:T(8,128)}, ...) | async-done | bytes 7077904 | tf_op jit(solution)/shard_map/psum | solution.py:254
  652.6 12.8 %all-to-all-done.7 = bf16[16,2,4,16,384]{4,2,1,0,3:T(4,128)(2,1)} async-done(((bf16[16,2,4,16,384]{4,2,1,0,3:T(4,128)(2,1)}), bf16[16,2,4,16,384]{4,2,1,0,3:T(4,128)(2,1)}, u32[]{:S(2)}, u32[]{:S(2)}) %all-to-all-start.7) | async-done | bytes 1572896 | tf_op jit(solution)/shard_map/all_to_all | solution.py:236
  (197 shorter events, 263.9 us)
Async XLA Ops:
  7.2 219.1 %copy-start = (bf16[384,1536]{1,0:T(8,128)(2,1)S(1)}, bf16[384,1536]{1,0:T(8,128)(2,1)}, u32[]{:S(2)}) copy-start(bf16[384,1536]{1,0:T(8,128)(2,1)} %param.18) | copy-start | bytes 3538948
  10.1 43.3 %all-to-all-start = ((bf16[16,16,4,2,384]{4,1,3,2,0:T(8,128)(2,1)}), bf16[16,16,4,2,384]{4,1,3,2,0:T(8,128)(2,1)S(1)}, u32[]{:S(2)}, u32[]{:S(2)}) async-start(bf16[16,16,4,2,384]{4,1,3,2,0:T(8,128)(2,1)} %copy.132), calls=%async_computation | async-start | bytes 3145728 | tf_op jit(solution)/shard_map/all_to_all | solution.py:194
  54.5 40.1 %all-to-all-start.4 = ((bf16[16,16,4,2,384]{4,1,3,2,0:T(8,128)(2,1)}), bf16[16,16,4,2,384]{4,1,3,2,0:T(8,128)(2,1)S(1)}, u32[]{:S(2)}, u32[]{:S(2)}) async-start(bf16[16,16,4,2,384]{4,1,3,2,0:T(8,128)(2,1)} %copy.151), calls=%async_computation.4 | async-start | bytes 3145728 | tf_op jit(solution)/shard_map/all_to_all | solution.py:201
  95.7 24.7 %all-to-all-start.1 = ((bf16[4,16,16,2,384]{4,3,2,0,1:T(2,128)(2,1)}), bf16[4,16,16,2,384]{4,3,2,0,1:T(2,128)(2,1)S(1)}, u32[]{:S(2)}, u32[]{:S(2)}) async-start(bf16[4,16,16,2,384]{4,3,2,0,1:T(2,128)(2,1)} %copy.134), calls=%async_computation.1 | async-start | bytes 3145728 | tf_op jit(solution)/shard_map/all_to_all | solution.py:193
  120.5 25.9 %all-to-all-start.5 = ((bf16[4,16,16,2,384]{4,3,2,0,1:T(2,128)(2,1)}), bf16[4,16,16,2,384]{4,3,2,0,1:T(2,128)(2,1)}, u32[]{:S(2)}, u32[]{:S(2)}) async-start(bf16[4,16,16,2,384]{4,3,2,0,1:T(2,128)(2,1)} %copy.153), calls=%async_computation.5 | async-start | bytes 3145728 | tf_op jit(solution)/shard_map/all_to_all | solution.py:200
  131.4 23.8 %copy-start.20 = (f32[2048]{0:T(1024)}, f32[2048]{0:T(1024)S(1)}, u32[]{:S(2)}) copy-start(f32[2048]{0:T(1024)S(1)} %rsqrt.21) | copy-start | bytes 24580
  132.7 22.5 %copy-start.22 = (f32[2048]{0:T(1024)}, f32[2048]{0:T(1024)S(1)}, u32[]{:S(2)}) copy-start(f32[2048]{0:T(1024)S(1)} %div.43) | copy-start | bytes 24580
  148.0 7.2 %copy-start.25 = (f32[384]{0:T(512)S(1)}, f32[384]{0:T(512)}, u32[]{:S(2)}) copy-start(f32[384]{0:T(512)} %param.14) | copy-start | bytes 4612
  225.5 25.8 %copy-start.2 = (f32[2048,384]{1,0:T(8,128)}, f32[2048,384]{1,0:T(8,128)S(1)}, u32[]{:S(2)}) copy-start(f32[2048,384]{1,0:T(8,128)S(1)} %get-tuple-element.128) | copy-start | bytes 9437188
  251.3 6.3 copy-start.18
  251.3 6.3 copy-start.19
  261.3 7.3 %copy-start.8 = (bf16[2048,384]{1,0:T(8,128)(2,1)S(1)}, bf16[2048,384]{1,0:T(8,128)(2,1)}, u32[]{:S(2)}) copy-start(bf16[2048,384]{1,0:T(8,128)(2,1)} %reshape.158) | copy-start | bytes 4718596
  264.2 178.2 %all-to-all-start.2 = ((bf16[4,2,16,16,384]{4,3,1,0,2:T(8,128)(2,1)}), bf16[4,2,16,16,384]{4,3,1,0,2:T(8,128)(2,1)}, u32[]{:S(2)}, u32[]{:S(2)}) async-start(bf16[4,2,16,16,384]{4,3,1,0,2:T(8,128)(2,1)} %copy.144), calls=%async_computation.2 | async-start | bytes 3145728 | tf_op jit(solution)/shard_map/all_to_all | solution.py:224
  268.5 368.4 %all-reduce.4.cloned.1.call-start = ((), (), s32[]{:S(2)}) async-start(), calls=%async_computation.8 | async-start | bytes 14155776 | tf_op jit(solution)/shard_map/psum | solution.py:254
  268.6 6.4 copy-start.15
  422.5 6.4 copy-start.4
  422.5 6.4 copy-start.13
  432.0 7.3 %copy-start.5 = (f32[2048,384]{1,0:T(8,128)S(1)}, f32[2048,384]{1,0:T(8,128)}, u32[]{:S(2)}) copy-start(f32[2048,384]{1,0:T(8,128)} %copy-done.3) | copy-start | bytes 9437188
  432.0 7.3 %copy-start.6 = (f32[2048,384]{1,0:T(8,128)S(1)}, f32[2048,384]{1,0:T(8,128)}, u32[]{:S(2)}) copy-start(f32[2048,384]{1,0:T(8,128)} %reshape.160) | copy-start | bytes 9437188
  442.4 57.9 %all-to-all-start.6 = ((bf16[4,2,16,16,384]{4,3,1,0,2:T(8,128)(2,1)}), bf16[4,2,16,16,384]{4,3,1,0,2:T(8,128)(2,1)S(1)}, u32[]{:S(2)}, u32[]{:S(2)}) async-start(bf16[4,2,16,16,384]{4,3,1,0,2:T(8,128)(2,1)} %copy.159), calls=%async_computation.6 | async-start | bytes 3145728 | tf_op jit(solution)/shard_map/all_to_all | solution.py:237
  449.1 56.0 %copy-start.27 = (f32[384]{0:T(512)S(1)}, f32[384]{0:T(512)}, u32[]{:S(2)}) copy-start(f32[384]{0:T(512)} %get-tuple-element.91) | copy-start | bytes 4612
  501.5 138.3 %all-to-all-start.3 = ((bf16[16,2,4,16,384]{4,2,1,0,3:T(4,128)(2,1)}), bf16[16,2,4,16,384]{4,2,1,0,3:T(4,128)(2,1)S(1)}, u32[]{:S(2)}, u32[]{:S(2)}) async-start(bf16[16,2,4,16,384]{4,2,1,0,3:T(4,128)(2,1)} %copy.147), calls=%async_computation.3 | async-start | bytes 3145728 | tf_op jit(solution)/shard_map/all_to_all | solution.py:223
  636.9 7.4 %copy-start.16 = (f32[384,384]{1,0:T(8,128)S(1)}, f32[384,384]{1,0:T(8,128)}, u32[]{:S(2)}) copy-start(f32[384,384]{1,0:T(8,128)} %get-tuple-element.114) | copy-start | bytes 1769476
  639.8 25.5 %all-to-all-start.7 = ((bf16[16,2,4,16,384]{4,2,1,0,3:T(4,128)(2,1)}), bf16[16,2,4,16,384]{4,2,1,0,3:T(4,128)(2,1)}, u32[]{:S(2)}, u32[]{:S(2)}) async-start(bf16[16,2,4,16,384]{4,2,1,0,3:T(4,128)(2,1)} %copy.162), calls=%async_computation.7 | async-start | bytes 3145728 | tf_op jit(solution)/shard_map/all_to_all | solution.py:236
  (15 other events, 30.8 us)
Sparse Core Ops, SparseCore 0:
  430.9 205.9 all-reduce.3
where the time goes:
time: 682 us; the launch traced here: 676 us
  matrix products  226 us (33%)
  waiting for transfers between devices  220 us (32%)
  local copies, waits for them, and re-layouts  101 us (15%)
  blocking collectives  57.2 us (8%)
  starting transfers between devices  36 us (5%)
  other arithmetic  20 us (3%)
  between operations  14.8 us (2%)
    psum x1, waiting for transfers between devices, shards(): lax.psum((grad_joint, grad_out, grad_up, grad_down, grad_first, grad_seco...  69.9 us
    psum x1, blocking collectives, shards(): lax.psum((grad_joint, grad_out, grad_up, grad_down, grad_first, grad_seco...  57.2 us
    all_to_all x1, waiting for transfers between devices, shards(): lax.all_to_all(regroup(grad_input.reshape(-1, tokens, channels)), 'row',...  49.4 us
    sub x8, matrix products, attend(): weights = jnp.exp(scores - row_max)  45.4 us
    dot_general x4, matrix products, attend_backward(): jnp.einsum('bhqk,bkhe->bqhe', grad_scores, key_rows, preferred_element_ty...  40 us
    dot_general x4, matrix products, attend_backward(): jnp.einsum('bhqk,bqhe->bkhe', grad_scores, queries, preferred_element_typ...  37.1 us
    all_to_all x1, waiting for transfers between devices, shards(): lax.all_to_all(to_layout(activations), 'row', split_axis=0, concat_axis=2...  34.2 us
    all_to_all x1, waiting for transfers between devices, shards(): lax.all_to_all(to_layout(cotangent), 'row', split_axis=0, concat_axis=2,...  32.3 us
  transfers between devices with their start and end apart: 9, of which 7 were waited for; matrix products, arithmetic and copies ran while one was open for 32% of the time, Pallas kernels for 0%

commit v1 on v0

v1 whole, which is shorter than its diff:
```python
import functools

import jax
import jax.numpy as jnp
from jax import lax
from jax.experimental import pallas as pl
from jax.experimental.pallas import tpu as pltpu
from jax.sharding import PartitionSpec as P

HEADS = 12
GRID = 16
SUB = 8
EPSILON = 1e-05
INV_ROOT_TAU = 0.3989422804014327
SQRT_HALF = 0.7071067811865476
LOG2E = 1.4426950408889634
BF = jnp.bfloat16
F32 = jnp.float32

ERFC_P = 0.4
ERFC_C = (
    0.2256758624069583,
    0.22566957331484927,
    0.20784305752189558,
    0.16853970978283367,
    0.1414388899580775,
    -0.005621196233437842,
    0.16909944767289115,
    -0.18290897174728507,
    0.05026375199644912,
)


def nn(a, b):
    return lax.dot_general(a, b, (((1,), (0,)), ((), ())), preferred_element_type=F32)


def nt(a, b):
    return lax.dot_general(a, b, (((1,), (1,)), ((), ())), preferred_element_type=F32)


def tn(a, b):
    return lax.dot_general(a, b, (((0,), (0,)), ((), ())), preferred_element_type=F32)


def gelu_parts(pre):
    gauss = jnp.exp2(pre * pre * (-0.5 * LOG2E))
    t = 1.0 / (1.0 + (ERFC_P * SQRT_HALF) * jnp.abs(pre))
    poly = jnp.full_like(t, 0.5 * ERFC_C[-1])
    for coef in ERFC_C[-2::-1]:
        poly = poly * t + 0.5 * coef
    half_erfc = gauss * (t * poly)
    phi = jnp.where(pre < 0.0, half_erfc, 1.0 - half_erfc)
    return phi, gauss


def normalize(values):
    center = values - jnp.mean(values, axis=0, keepdims=True)
    inv_std = lax.rsqrt(jnp.mean(center * center, axis=0, keepdims=True) + EPSILON)
    return center * inv_std, inv_std


def norm_back(scaled, normed, inv_std):
    return inv_std * (
        scaled
        - jnp.mean(scaled, axis=0, keepdims=True)
        - normed * jnp.mean(scaled * normed, axis=0, keepdims=True)
    )


def load_rows(ref):
    pieces, _, sub, width = ref.shape
    return ref[...].reshape(pieces, sub, width).astype(F32).reshape(pieces * sub, width)


def store_rows(ref, rows):
    pieces, _, sub, width = ref.shape
    ref[...] = rows.reshape(pieces, 1, sub, width).astype(ref.dtype)


def fold_lanes(values):
    total = values[:, :128]
    for start in range(128, values.shape[1], 128):
        total = total + values[:, start : start + 128]
    return total


def attend_kernel(act_ref, gain_ref, joint_ref, flat_ref, triple_ref, mixed_ref):
    width = gain_ref.shape[0]
    head = width // HEADS
    factor = head ** (-0.5) * LOG2E
    flat = load_rows(act_ref).T
    flat_ref[0] = flat.astype(BF)
    normed, _ = normalize(flat)
    scaled = (normed * gain_ref[...]).astype(BF)
    triple_ref[0] = nn(joint_ref[...], scaled).astype(BF)
    for h in range(HEADS):
        rows = slice(h * head, (h + 1) * head)
        queries = triple_ref[0, h * head : (h + 1) * head]
        keys = triple_ref[0, width + h * head : width + (h + 1) * head]
        values = triple_ref[0, 2 * width + h * head : 2 * width + (h + 1) * head]
        scores = tn(keys, queries)
        weights = jnp.exp2((scores - jnp.max(scores, axis=0, keepdims=True)) * factor)
        weights = weights * (1.0 / jnp.sum(weights, axis=0, keepdims=True))
        mixed_ref[0, rows] = nn(values, weights.astype(BF)).astype(BF)


def mlp_kernel(
    flat_ref, mixed_ref, cot_ref, gain_ref, out_t_ref, up_t_ref, down_t_ref, down_ref, up_ref, out_w_ref,
    result_ref, grad_att_ref, grad_mixed_ref, grads_ref, grad_gain_ref,
    acc_ref,
):
    step = pl.program_id(0)
    width = gain_ref.shape[0]
    hidden_dim = up_ref.shape[1]

    @pl.when(step == 0)
    def _():
        acc_ref[...] = jnp.zeros_like(acc_ref)
        grad_gain_ref[...] = jnp.zeros_like(grad_gain_ref)

    cot_rows = load_rows(cot_ref)
    cot_b = cot_rows.astype(BF)
    cot_t = cot_rows.T
    cot_tb = cot_t.astype(BF)
    mixed = mixed_ref[0]
    attended = flat_ref[0].astype(F32) + nn(out_t_ref[...], mixed)
    normed, inv_std = normalize(attended)
    gain = gain_ref[...]
    scaled = (normed * gain).astype(BF)
    result = attended
    grad_scaled = jnp.zeros_like(attended)
    piece = width
    for start in range(0, hidden_dim, piece):
        part = slice(start, start + piece)
        pre = nn(up_t_ref[part], scaled)
        phi, gauss = gelu_parts(pre)
        hidden = (pre * phi).astype(BF)
        result = result + nn(down_t_ref[:, part], hidden)
        acc_ref[part] += nn(hidden, cot_b)
        grad_hidden = nn(down_ref[part], cot_tb).astype(BF).astype(F32)
        grad_pre = (grad_hidden * (phi + pre * gauss * INV_ROOT_TAU)).astype(BF)
        grad_scaled = grad_scaled + nn(up_ref[:, part], grad_pre)
        acc_ref[hidden_dim + start : hidden_dim + start + piece] += nt(grad_pre, scaled)
    store_rows(result_ref, result.T)
    grad_gain_ref[...] += fold_lanes(grad_scaled * normed)
    grad_att = cot_t + norm_back(grad_scaled * gain, normed, inv_std)
    grad_att_ref[0] = grad_att
    grad_att_b = grad_att.astype(BF)
    acc_ref[2 * hidden_dim :] += nt(mixed, grad_att_b)
    grad_mixed_ref[0] = nn(out_w_ref[...], grad_att_b).astype(BF)

    @pl.when(step == pl.num_programs(0) - 1)
    def _():
        grads_ref[...] = acc_ref[...].astype(BF)


def back_kernel(
    flat_ref, triple_ref, grad_mixed_ref, grad_att_ref, gain_ref, joint_ref,
    grad_in_ref, grads_ref, grad_gain_ref,
    acc_ref, grad_triple_ref,
):
    step = pl.program_id(0)
    width = gain_ref.shape[0]
    head = width // HEADS
    scale = head ** (-0.5)

    @pl.when(step == 0)
    def _():
        acc_ref[...] = jnp.zeros_like(acc_ref)
        grad_gain_ref[...] = jnp.zeros_like(grad_gain_ref)

    for h in range(HEADS):
        queries = triple_ref[0, h * head : (h + 1) * head]
        keys = triple_ref[0, width + h * head : width + (h + 1) * head]
        values = triple_ref[0, 2 * width + h * head : 2 * width + (h + 1) * head]
        grad_heads = grad_mixed_ref[0, h * head : (h + 1) * head]
        scores = tn(keys, queries)
        weights = jnp.exp2((scores - jnp.max(scores, axis=0, keepdims=True)) * (scale * LOG2E))
        weights = weights * (1.0 / jnp.sum(weights, axis=0, keepdims=True))
        grad_weights = tn(values, grad_heads)
        inner = jnp.sum(weights * grad_weights, axis=0, keepdims=True)
        grad_scores = (weights * (grad_weights - inner) * scale).astype(BF)
        grad_triple_ref[h * head : (h + 1) * head] = nn(keys, grad_scores).astype(BF)
        grad_triple_ref[width + h * head : width + (h + 1) * head] = nt(queries, grad_scores).astype(BF)
        grad_triple_ref[2 * width + h * head : 2 * width + (h + 1) * head] = nt(
            grad_heads, weights.astype(BF)
        ).astype(BF)
    normed, inv_std = normalize(flat_ref[0].astype(F32))
    gain = gain_ref[...]
    scaled = (normed * gain).astype(BF)
    acc_ref[...] += nt(grad_triple_ref[...], scaled)
    grad_scaled = nn(joint_ref[...], grad_triple_ref[...])
    grad_gain_ref[...] += fold_lanes(grad_scaled * normed)
    grad_in = grad_att_ref[0] + norm_back(grad_scaled * gain, normed, inv_std)
    store_rows(grad_in_ref, grad_in.T)

    @pl.when(step == pl.num_programs(0) - 1)
    def _():
        grads_ref[...] = acc_ref[...].astype(BF)


def whole(array):
    return pl.BlockSpec(array.shape, lambda g: (0,) * array.ndim)


def per_group(shape):
    return pl.BlockSpec((1,) + shape, lambda g: (g, 0, 0))


def pieces_spec(array):
    pieces, _, sub, width = array.shape
    return pl.BlockSpec((pieces, 1, sub, width), lambda g: (0, g, 0, 0))


def params():
    return pltpu.CompilerParams(dimension_semantics=("arbitrary",), vmem_limit_bytes=60 << 20)


def cost(flops, bytes_moved, exps):
    return pl.CostEstimate(flops=int(flops), bytes_accessed=int(bytes_moved), transcendentals=int(exps))


def attend_call(act, gain, joint_t):
    pieces, groups, sub, width = act.shape
    tokens = pieces * sub
    return pl.pallas_call(
        attend_kernel,
        grid=(groups,),
        in_specs=[pieces_spec(act), whole(gain), whole(joint_t)],
        out_specs=[per_group((width, tokens)), per_group((3 * width, tokens)), per_group((width, tokens))],
        out_shape=[
            jax.ShapeDtypeStruct((groups, width, tokens), BF),
            jax.ShapeDtypeStruct((groups, 3 * width, tokens), BF),
            jax.ShapeDtypeStruct((groups, width, tokens), BF),
        ],
        compiler_params=params(),
        cost_estimate=cost(3e9 * groups, 12 * groups * tokens * width, 0),
    )(act, gain, joint_t)


def mlp_call(flat, mixed, cot, gain, weights):
    pieces, groups, sub, width = cot.shape
    tokens = pieces * sub
    hidden_dim = weights[1].shape[0]
    rows = 2 * hidden_dim + width
    return pl.pallas_call(
        mlp_kernel,
        grid=(groups,),
        in_specs=[per_group((width, tokens)), per_group((width, tokens)), pieces_spec(cot), whole(gain)]
        + [whole(w) for w in weights],
        out_specs=[
            pieces_spec(cot),
            per_group((width, tokens)),
            per_group((width, tokens)),
            pl.BlockSpec((rows, width), lambda g: (0, 0)),
            pl.BlockSpec((width, 128), lambda g: (0, 0)),
        ],
        out_shape=[
            jax.ShapeDtypeStruct(cot.shape, BF),
            jax.ShapeDtypeStruct((groups, width, tokens), F32),
            jax.ShapeDtypeStruct((groups, width, tokens), BF),
            jax.ShapeDtypeStruct((rows, width), BF),
            jax.ShapeDtypeStruct((width, 128), F32),
        ],
        scratch_shapes=[pltpu.VMEM((rows, width), F32)],
        compiler_params=params(),
        cost_estimate=cost(4e9 * groups, 14 * groups * tokens * width, 0),
    )(flat, mixed, cot, gain, *weights)


def back_call(flat, triple, grad_mixed, grad_att, gain, joint, like):
    pieces, groups, sub, width = like.shape
    tokens = pieces * sub
    return pl.pallas_call(
        back_kernel,
        grid=(groups,),
        in_specs=[
            per_group((width, tokens)),
            per_group((3 * width, tokens)),
            per_group((width, tokens)),
            per_group((width, tokens)),
            whole(gain),
            whole(joint),
        ],
        out_specs=[
            pieces_spec(like),
            pl.BlockSpec((3 * width, width), lambda g: (0, 0)),
            pl.BlockSpec((width, 128), lambda g: (0, 0)),
        ],
        out_shape=[
            jax.ShapeDtypeStruct(like.shape, BF),
            jax.ShapeDtypeStruct((3 * width, width), BF),
            jax.ShapeDtypeStruct((width, 128), F32),
        ],
        scratch_shapes=[pltpu.VMEM((3 * width, width), F32), pltpu.VMEM((3 * width, tokens), BF)],
        compiler_params=params(),
        cost_estimate=cost(6e9 * groups, 18 * groups * tokens * width, 0),
    )(flat, triple, grad_mixed, grad_att, gain, joint)


def shards(
    activations,
    cotangent,
    first_gain,
    joint_weight,
    output_weight,
    second_gain,
    expand_weight,
    reduce_weight,
):
    row_devs = lax.axis_size("row")
    col_devs = lax.axis_size("col")
    devices = row_devs * col_devs
    both = ("row", "col")
    tile_rows, tile_cols, channels = activations.shape
    local_rows = GRID // row_devs
    local_cols = GRID // col_devs
    stride_rows = tile_rows // local_rows
    stride_cols = tile_cols // local_cols
    part_rows = stride_rows // row_devs
    part_cols = stride_cols // col_devs
    groups = part_rows * part_cols
    share = local_rows * local_cols
    tokens = GRID * GRID
    factor = float(tile_rows * tile_cols * devices) ** (-0.5)

    def scatter(tile):
        sends = tile.reshape(
            local_rows, row_devs, part_rows, local_cols, col_devs, part_cols, channels
        ).transpose(1, 4, 2, 5, 0, 3, 6).reshape(devices, groups, share, channels)
        got = lax.all_to_all(sends, both, split_axis=0, concat_axis=0, tiled=True)
        if share % SUB:
            got = got.transpose(0, 2, 1, 3).reshape(tokens // SUB, SUB, groups, channels).transpose(0, 2, 1, 3)
        return got.reshape(tokens // SUB, groups, SUB, channels)

    def gather(pieces):
        if share % SUB:
            pieces = pieces.transpose(0, 2, 1, 3).reshape(devices, share, groups, channels).transpose(0, 2, 1, 3)
        got = lax.all_to_all(
            pieces.reshape(devices, groups, share, channels), both, split_axis=0, concat_axis=0, tiled=True
        )
        return got.reshape(
            row_devs, col_devs, part_rows, part_cols, local_rows, local_cols, channels
        ).transpose(4, 0, 2, 5, 1, 3, 6).reshape(tile_rows, tile_cols, channels)

    def total(partial):
        rows, width = partial.shape
        by_col = rows // col_devs
        by_row = by_col // row_devs
        got = lax.all_to_all(partial.reshape(col_devs, by_col, width), "col", 0, 0, tiled=True)
        mine = jnp.sum(got.astype(F32), axis=0).astype(BF)
        got = lax.all_to_all(mine.reshape(row_devs, by_row, width), "row", 0, 0, tiled=True)
        mine = jnp.sum(got.astype(F32), axis=0).astype(BF)
        got = lax.all_to_all(
            jnp.broadcast_to(mine[None], (row_devs, by_row, width)), "row", 0, 0, tiled=True
        ).reshape(by_col, width)
        got = lax.all_to_all(
            jnp.broadcast_to(got[None], (col_devs, by_col, width)), "col", 0, 0, tiled=True
        )
        return got.reshape(rows, width).astype(F32) * factor

    def spread(gain):
        return jnp.broadcast_to(gain[:, None], (channels, tokens))

    act = scatter(activations)
    cot = scatter(cotangent)
    gain_one, gain_two = spread(first_gain), spread(second_gain)
    flat, triple, mixed = attend_call(act, gain_one, joint_weight.T)
    result, grad_att, grad_mixed, tail_grads, grad_second = mlp_call(
        flat,
        mixed,
        cot,
        gain_two,
        (output_weight.T, expand_weight.T, reduce_weight.T, reduce_weight, expand_weight, output_weight),
    )
    block_out = gather(result)
    tail_sum = total(tail_grads)
    grad_in, head_grads, grad_first = back_call(
        flat, triple, grad_mixed, grad_att, gain_one, joint_weight, cot
    )
    grad_input = gather(grad_in)
    head_sum = total(head_grads)
    gains = jnp.stack([jnp.sum(grad_first, axis=1), jnp.sum(grad_second, axis=1)])
    gains = lax.all_to_all(
        jnp.broadcast_to(gains[None], (devices,) + gains.shape), both, 0, 0, tiled=True
    )
    gains = jnp.sum(gains, axis=0) * factor
    hidden_dim = expand_weight.shape[1]
    return (
        block_out,
        grad_input,
        head_sum.T,
        tail_sum[2 * hidden_dim :],
        tail_sum[hidden_dim : 2 * hidden_dim].T,
        tail_sum[:hidden_dim],
        gains[0],
        gains[1],
    )


def solution(mesh):
    placed = (P("row", "col", None), P("row", "col", None), P(), P(), P(), P(), P(), P())
    return jax.shard_map(
        shards,
        mesh=mesh,
        in_specs=placed,
        out_specs=placed,
        check_vma=False,
    )
```

time: 682 us -> 459 us (0.67)
  matrix products: 226 us -> 0 us
  Pallas kernels: 0 us -> 138 us
  waiting for transfers between devices: 220 us -> 166 us
  local copies, waits for them, and re-layouts: 101 us -> 59.5 us
  other arithmetic: 20 us -> 4.56 us
  between operations: 14.8 us -> 0.89 us
    dot_general x32 -> x0, matrix products: 181 us -> none  [the longest x4 40 us: attend_backward(): jnp.einsum('bhqk,bkhe->bqhe', grad_scores, key_rows, preferred_element_ty...]
    pallas_call x0 -> x3, Pallas kernels: none -> 138 us  [the longest x1 50 us: mlp_call(): pl.pallas_call(mlp_kernel, grid=(groups,), in_specs=[per_group((width, to...]
    psum x1 -> x0, waiting for transfers between devices: 69.9 us -> none  [shards(): lax.psum((grad_joint, grad_out, grad_up, grad_down, grad_first, grad_seco...]
    psum x1 -> x0, blocking collectives: 57.2 us -> none  [shards(): lax.psum((grad_joint, grad_out, grad_up, grad_down, grad_first, grad_seco...]
    all_to_all x0 -> x4, blocking collectives: none -> 50.6 us  [the longest x2 22.1 us: total(): lax.all_to_all(jnp.broadcast_to(mine[None], (row_devs, by_row, width)), '...]
    sub x8 -> x0, matrix products: 45.4 us -> none  [attend(): weights = jnp.exp(scores - row_max)]
    reshape x1 -> x12, local copies, waits for them, and re-layouts: 4.79 us -> 30.5 us  [the longest x2 9.28 us: gather(): return got.reshape(row_devs, col_devs, part_rows, part_cols, local_rows,...]
    all_to_all x15 -> x0, local copies, waits for them, and re-layouts: 23.4 us -> none  [the longest x2 4.18 us: shards(): lax.all_to_all(to_layout(activations), 'row', split_axis=0, concat_axis=2...]
  transfers between devices with their start and end apart: 9 -> 9, of which waited for: 7 -> 7; matrix products, arithmetic and copies ran while one was open for 32% -> 10% of each run, Pallas kernels for 0% -> 8%
where the time goes in v1:
time: 459 us; the launch traced here: 457 us
  waiting for transfers between devices  166 us (36%)
  Pallas kernels  138 us (30%)
  local copies, waits for them, and re-layouts  59.5 us (13%)
  blocking collectives  50.6 us (11%)
  starting transfers between devices  37.7 us (8%)
    all_to_all x2, waiting for transfers between devices, gather(): lax.all_to_all(pieces.reshape(devices, groups, share, channels), both, sp...  75.1 us
    pallas_call x1, Pallas kernels, mlp_call(): pl.pallas_call(mlp_kernel, grid=(groups,), in_specs=[per_group((width, to...  50 us
    pallas_call x1, Pallas kernels, back_call(): pl.pallas_call(back_kernel, grid=(groups,), in_specs=[per_group((width, t...  49.3 us
    pallas_call x1, Pallas kernels, attend_call(): pl.pallas_call(attend_kernel, grid=(groups,), in_specs=[pieces_spec(act),...  38.8 us
    all_to_all x2, waiting for transfers between devices, scatter(): got = lax.all_to_all(sends, both, split_axis=0, concat_axis=0, tiled=True)  33.8 us
    all_to_all x1, waiting for transfers between devices, total(): lax.all_to_all(partial.reshape(col_devs, by_col, width), 'col', 0, 0, til...  32.5 us
    all_to_all x2, blocking collectives, total(): lax.all_to_all(jnp.broadcast_to(mine[None], (row_devs, by_row, width)), '...  22.1 us
    all_to_all x1, blocking collectives, total(): lax.all_to_all(partial.reshape(col_devs, by_col, width), 'col', 0, 0, til...  17.5 us
  transfers between devices with their start and end apart: 9, of which 7 were waited for; matrix products, arithmetic and copies ran while one was open for 10% of the time, Pallas kernels for 8%

profile of v1, /device:TPU:0, one launch (start us, length us, event | category | flops | bytes accessed | tf_op | source)
XLA Modules:
  0.0 457.5 jit_solution(295268380232256967)
XLA Ops:
  7.4 7.4 %all-to-all-start = ((bf16[32,8,8,384]{3,2,1,0:T(8,128)(2,1)}), bf16[32,8,8,384]{3,2,1,0:T(8,128)(2,1)}, u32[]{:S(2)}, u32[]{:S(2)}) async-start(bf16[32,8,8,384]{3,2,1,0:T(8,128)(2,1)} %reshape.68), calls=%async_computation | async-start | bytes 3145728 | tf_op jit(solution)/shard_map/all_to_all | solution.py:332
  18.7 33.8 %all-to-all-done.act_ref = bf16[32,8,8,384]{3,2,1,0:T(8,128)(2,1)} async-done(((bf16[32,8,8,384]{3,2,1,0:T(8,128)(2,1)}), bf16[32,8,8,384]{3,2,1,0:T(8,128)(2,1)}, u32[]{:S(2)}, u32[]{:S(2)}) %all-to-all-start) | async-done | bytes 1572896 | tf_op jit(solution)/shard_map/all_to_all | solution.py:332
  52.4 4.0 all-to-all-start.1
  64.3 38.8 %shard_map.143 = (bf16[8,384,256]{2,1,0:T(8,128)(2,1)}, bf16[8,1152,256]{2,1,0:T(8,128)(2,1)}, bf16[8,384,256]{2,1,0:T(8,128)(2,1)}) custom-call(bf16[32,8,8,384]{3,2,1,0:T(8,128)(2,1)} %all-to-all-done.act_ref, f32[384,256]{1,0:T(8,128)} %broadcast_in_dim.18.gain_ref, bf16[1152,384]{1,0:T(8,128)(2,1)} %bitcast.35), custom_call_target="tpu_custom_call" | custom-call | flops 24000000000 | bytes 9437184 | tf_op jit(solution)/shard_map/pallas_call | solution.py:227
  104.4 50.0 %shard_map.144 = (bf16[32,8,8,384]{3,2,1,0:T(8,128)(2,1)}, f32[8,384,256]{2,1,0:T(8,128)}, bf16[8,384,256]{2,1,0:T(8,128)(2,1)}, bf16[3456,384]{1,0:T(8,128)(2,1)}, f32[384,128]{1,0:T(8,128)}) custom-call(bf16[8,384,256]{2,1,0:T(8,128)(2,1)} %get-tuple-element.19.flat_ref, bf16[8,384,256]{2,1,0:T(8,128)(2,1)} %get-tuple-element.20.mixed_ref, ...), custom_call_target="tpu_custom_call" | custom-call | flops 32000000000 | bytes 11010048 | tf_op jit(solution)/shard_map/pallas_call | solution.py:247
  154.4 49.3 %shard_map.145 = (bf16[32,8,8,384]{3,2,1,0:T(8,128)(2,1)}, bf16[1152,384]{1,0:T(8,128)(2,1)}, f32[384,128]{1,0:T(8,128)}) custom-call(bf16[8,384,256]{2,1,0:T(8,128)(2,1)} %get-tuple-element.19.flat_ref, bf16[8,1152,256]{2,1,0:T(8,128)(2,1)} %get-tuple-element.22.triple_ref, bf16[8,384,256]{2,1,0:T(8,128)(2,1)} %get-tuple-element.23.grad_mixed_ref, ...), custom_call_target="tpu_custom_call" | custom-call | flops 48000000000 | bytes 14155776 | tf_op jit(solution)/shard_map/pallas_call | solution.py:275
  203.7 17.5 %all_to_all.65 = bf16[8,144,384]{2,1,0:T(8,128)(2,1)S(1)} all-to-all(bf16[8,144,384]{2,1,0:T(8,128)(2,1)} %bitcast.34), channel_id=1, replica_groups=mesh['row'=4,'col'=8] {'col'}, dimensions={0} | all-to-all | bytes 1769472 | tf_op jit(solution)/shard_map/all_to_all | solution.py:351
  222.0 4.6 %all-to-all-start.5 = ((bf16[4,36,384]{2,1,0:T(8,128)(2,1)}), bf16[4,36,384]{2,1,0:T(8,128)(2,1)S(1)}, u32[]{:S(2)}, u32[]{:S(2)}) async-start(bf16[4,36,384]{2,1,0:T(8,128)(2,1)} %reshape.76), calls=%async_computation.5 | async-start | bytes 245760 | tf_op jit(solution)/shard_map/all_to_all | solution.py:353
  227.0 5.6 %all-to-all-done.5 = bf16[4,36,384]{2,1,0:T(8,128)(2,1)S(1)} async-done(((bf16[4,36,384]{2,1,0:T(8,128)(2,1)}), bf16[4,36,384]{2,1,0:T(8,128)(2,1)S(1)}, u32[]{:S(2)}, u32[]{:S(2)}) %all-to-all-start.5) | async-done | bytes 110624 | tf_op jit(solution)/shard_map/all_to_all | solution.py:353
  235.8 7.8 %all-to-all-done.12 = f32[32,2,384]{2,1,0:T(2,128)S(1)} async-done(((f32[32,2,384]{2,1,0:T(2,128)}), f32[32,2,384]{2,1,0:T(2,128)S(1)}, u32[]{:S(2)}, u32[]{:S(2)}) %all-to-all-start.12) | async-done | bytes 98336 | tf_op jit(solution)/shard_map/all_to_all | solution.py:385
  243.6 8.7 %all_to_all.66 = bf16[4,36,384]{2,1,0:T(8,128)(2,1)S(1)} all-to-all(bf16[4,36,384]{2,1,0:T(8,128)(2,1)S(1)} %broadcast_in_dim.20), channel_id=1, replica_groups=mesh['row'=4,'col'=8] {'row'}, dimensions={0} | all-to-all | bytes 221184 | tf_op jit(solution)/shard_map/all_to_all | solution.py:355
  256.0 32.5 %all-to-all-done.8 = bf16[8,432,384]{2,1,0:T(8,128)(2,1)S(1)} async-done(((bf16[8,432,384]{2,1,0:T(8,128)(2,1)}), bf16[8,432,384]{2,1,0:T(8,128)(2,1)S(1)}, u32[]{:S(2)}, u32[]{:S(2)}) %all-to-all-start.8) | async-done | bytes 2654240 | tf_op jit(solution)/shard_map/all_to_all | solution.py:351
  295.2 11.4 %all-to-all-done.7 = bf16[8,144,384]{2,1,0:T(8,128)(2,1)S(1)} async-done(((bf16[8,144,384]{2,1,0:T(8,128)(2,1)}), bf16[8,144,384]{2,1,0:T(8,128)(2,1)S(1)}, u32[]{:S(2)}, u32[]{:S(2)}) %all-to-all-start.7) | async-done | bytes 884768 | tf_op jit(solution)/shard_map/all_to_all | solution.py:358
  306.6 11.0 %all_to_all.67 = bf16[4,108,384]{2,1,0:T(8,128)(2,1)S(1)} all-to-all(bf16[4,108,384]{2,1,0:T(8,128)(2,1)S(1)} %reshape.78), channel_id=1, replica_groups=mesh['row'=4,'col'=8] {'row'}, dimensions={0} | all-to-all | bytes 663552 | tf_op jit(solution)/shard_map/all_to_all | solution.py:353
  317.6 4.3 all-to-all-start.3
  321.9 37.6 %all-to-all-done.3 = bf16[32,8,8,384]{3,2,1,0:T(8,128)(2,1)S(1)} async-done(((bf16[32,8,8,384]{3,2,1,0:T(8,128)(2,1)}), bf16[32,8,8,384]{3,2,1,0:T(8,128)(2,1)S(1)}, u32[]{:S(2)}, u32[]{:S(2)}) %all-to-all-start.3) | async-done | bytes 1572896 | tf_op jit(solution)/shard_map/all_to_all | solution.py:340
  359.5 13.4 %all_to_all.68 = bf16[4,108,384]{2,1,0:T(8,128)(2,1)S(1)} all-to-all(bf16[4,108,384]{2,1,0:T(8,128)(2,1)S(1)} %broadcast_in_dim.23), channel_id=1, replica_groups=mesh['row'=4,'col'=8] {'row'}, dimensions={0} | all-to-all | bytes 663552 | tf_op jit(solution)/shard_map/all_to_all | solution.py:355
  376.8 37.6 %all-to-all-done.2 = bf16[32,8,8,384]{3,2,1,0:T(8,128)(2,1)S(1)} async-done(((bf16[32,8,8,384]{3,2,1,0:T(8,128)(2,1)}), bf16[32,8,8,384]{3,2,1,0:T(8,128)(2,1)S(1)}, u32[]{:S(2)}, u32[]{:S(2)}) %all-to-all-start.2) | async-done | bytes 1572896 | tf_op jit(solution)/shard_map/all_to_all | solution.py:340
  426.2 4.5 reshape.73
  430.7 4.1 copy.52
  434.8 4.6 %reshape.74 = bf16[64,32,384]{2,1,0:T(8,128)(2,1)} reshape(bf16[4,4,4,2,8,2,384]{6,5,4,3,2,1,0:T(2,128)(2,1)} %copy.52) | data formatting | bytes 3145728 | tf_op jit(solution)/shard_map/reshape | solution.py:345
  439.4 4.5 reshape.71
  443.9 4.1 copy.51
  448.0 4.6 %reshape.72 = bf16[64,32,384]{2,1,0:T(8,128)(2,1)} reshape(bf16[4,4,4,2,8,2,384]{6,5,4,3,2,1,0:T(2,128)(2,1)} %copy.51) | data formatting | bytes 3145728 | tf_op jit(solution)/shard_map/reshape | solution.py:345
  (72 shorter events, 55.0 us)
Async XLA Ops:
  7.4 7.5 %copy-start.3 = (bf16[64,32,384]{2,1,0:T(8,128)(2,1)S(1)}, bf16[64,32,384]{2,1,0:T(8,128)(2,1)}, u32[]{:S(2)}) copy-start(bf16[64,32,384]{2,1,0:T(8,128)(2,1)} %param.9) | copy-start | bytes 4718596
  7.4 45.1 %all-to-all-start = ((bf16[32,8,8,384]{3,2,1,0:T(8,128)(2,1)}), bf16[32,8,8,384]{3,2,1,0:T(8,128)(2,1)}, u32[]{:S(2)}, u32[]{:S(2)}) async-start(bf16[32,8,8,384]{3,2,1,0:T(8,128)(2,1)} %reshape.68), calls=%async_computation | async-start | bytes 3145728 | tf_op jit(solution)/shard_map/all_to_all | solution.py:332
  18.7 37.8 %copy-start.8 = (bf16[384,384]{1,0:T(8,128)(2,1)S(1)}, bf16[384,384]{1,0:T(8,128)(2,1)}, u32[]{:S(2)}) copy-start(bf16[384,384]{1,0:T(8,128)(2,1)} %out_w_ref.1) | copy-start | bytes 884740
  52.4 50.7 %all-to-all-start.1 = ((bf16[32,8,8,384]{3,2,1,0:T(8,128)(2,1)}), bf16[32,8,8,384]{3,2,1,0:T(8,128)(2,1)S(1)}, u32[]{:S(2)}, u32[]{:S(2)}) async-start(bf16[32,8,8,384]{3,2,1,0:T(8,128)(2,1)} %reshape.70), calls=%async_computation.1 | async-start | bytes 3145728 | tf_op jit(solution)/shard_map/all_to_all | solution.py:332
  56.4 3.1 copy-start.5
  61.0 2.5 copy-start.11
  64.3 38.8 %copy-start.12 = (f32[384]{0:T(512)S(1)}, f32[384]{0:T(512)}, u32[]{:S(2)}) copy-start(f32[384]{0:T(512)} %param.13) | copy-start | bytes 4612
  103.1 1.3 copy-start.4
  203.7 22.9 %copy-start.10 = (f32[384,128]{1,0:T(8,128)S(1)}, f32[384,128]{1,0:T(8,128)}, u32[]{:S(2)}) copy-start(f32[384,128]{1,0:T(8,128)} %get-tuple-element.28) | copy-start | bytes 589828
  203.7 23.1 %copy-start.9 = (f32[384,128]{1,0:T(8,128)S(1)}, f32[384,128]{1,0:T(8,128)}, u32[]{:S(2)}) copy-start(f32[384,128]{1,0:T(8,128)} %get-tuple-element.29) | copy-start | bytes 589828
  222.0 10.5 %all-to-all-start.5 = ((bf16[4,36,384]{2,1,0:T(8,128)(2,1)}), bf16[4,36,384]{2,1,0:T(8,128)(2,1)S(1)}, u32[]{:S(2)}, u32[]{:S(2)}) async-start(bf16[4,36,384]{2,1,0:T(8,128)(2,1)} %reshape.76), calls=%async_computation.5 | async-start | bytes 245760 | tf_op jit(solution)/shard_map/all_to_all | solution.py:353
  233.2 10.4 %all-to-all-start.12 = ((f32[32,2,384]{2,1,0:T(2,128)}), f32[32,2,384]{2,1,0:T(2,128)S(1)}, u32[]{:S(2)}, u32[]{:S(2)}) async-start(f32[32,2,384]{2,1,0:T(2,128)} %broadcast_in_dim.52), calls=%async_computation.12 | async-start | bytes 196608 | tf_op jit(solution)/shard_map/all_to_all | solution.py:385
  243.6 8.7 %copy-start.6 = (f32[32,2,384]{2,1,0:T(2,128)}, f32[32,2,384]{2,1,0:T(2,128)S(1)}, u32[]{:S(2)}) copy-start(f32[32,2,384]{2,1,0:T(2,128)S(1)} %all-to-all-done.12) | copy-start | bytes 294916
  252.3 36.2 %all-to-all-start.8 = ((bf16[8,432,384]{2,1,0:T(8,128)(2,1)}), bf16[8,432,384]{2,1,0:T(8,128)(2,1)S(1)}, u32[]{:S(2)}, u32[]{:S(2)}) async-start(bf16[8,432,384]{2,1,0:T(8,128)(2,1)} %bitcast.31), calls=%async_computation.8 | async-start | bytes 5308416 | tf_op jit(solution)/shard_map/all_to_all | solution.py:351
  289.4 17.1 %all-to-all-start.7 = ((bf16[8,144,384]{2,1,0:T(8,128)(2,1)}), bf16[8,144,384]{2,1,0:T(8,128)(2,1)S(1)}, u32[]{:S(2)}, u32[]{:S(2)}) async-start(bf16[8,144,384]{2,1,0:T(8,128)(2,1)} %broadcast_in_dim.22), calls=%async_computation.7 | async-start | bytes 1769472 | tf_op jit(solution)/shard_map/all_to_all | solution.py:358
  306.6 11.0 %copy-start.2 = (bf16[8,144,384]{2,1,0:T(8,128)(2,1)}, bf16[8,144,384]{2,1,0:T(8,128)(2,1)S(1)}, u32[]{:S(2)}) copy-start(bf16[8,144,384]{2,1,0:T(8,128)(2,1)S(1)} %all-to-all-done.7) | copy-start | bytes 2654212
  317.6 41.9 %all-to-all-start.3 = ((bf16[32,8,8,384]{3,2,1,0:T(8,128)(2,1)}), bf16[32,8,8,384]{3,2,1,0:T(8,128)(2,1)S(1)}, u32[]{:S(2)}, u32[]{:S(2)}) async-start(bf16[32,8,8,384]{3,2,1,0:T(8,128)(2,1)} %get-tuple-element.25), calls=%async_computation.3 | async-start | bytes 3145728 | tf_op jit(solution)/shard_map/all_to_all | solution.py:340
  359.5 13.5 %copy-start = (bf16[32,8,8,384]{3,2,1,0:T(8,128)(2,1)}, bf16[32,8,8,384]{3,2,1,0:T(8,128)(2,1)S(1)}, u32[]{:S(2)}) copy-start(bf16[32,8,8,384]{3,2,1,0:T(8,128)(2,1)S(1)} %all-to-all-done.3) | copy-start | bytes 4718596
  373.0 41.4 %all-to-all-start.2 = ((bf16[32,8,8,384]{3,2,1,0:T(8,128)(2,1)}), bf16[32,8,8,384]{3,2,1,0:T(8,128)(2,1)S(1)}, u32[]{:S(2)}, u32[]{:S(2)}) async-start(bf16[32,8,8,384]{3,2,1,0:T(8,128)(2,1)} %get-tuple-element.21), calls=%async_computation.2 | async-start | bytes 3145728 | tf_op jit(solution)/shard_map/all_to_all | solution.py:340
  414.4 2.0 copy-start.1
  416.3 4.0 copy-start.7
  416.4 36.3 %all-to-all-start.11 = ((bf16[8,432,384]{2,1,0:T(8,128)(2,1)}), bf16[8,432,384]{2,1,0:T(8,128)(2,1)S(1)}, u32[]{:S(2)}, u32[]{:S(2)}) async-start(bf16[8,432,384]{2,1,0:T(8,128)(2,1)} %broadcast_in_dim.25), calls=%async_computation.11 | async-start | bytes 5308416 | tf_op jit(solution)/shard_map/all_to_all | solution.py:358
